TPU v7x, 128 devices: a whole 4x4x4 slice. The times are simulated.
128 devices in a mesh: flow: 8 (over y, core), link: 16 (over x, z).
Axes of the slice: x: 4, y: 4, z: 4, core: 2. Of those that a mesh axis runs over, the one named last changes fastest.
Arguments:
- route_tiles: bfloat16 [1024, 2048, 128], P('flow', 'link'), may hold values from 0 to 1, as said below
- tile_count: int32 [8, 16], P('flow', 'link'), may hold values from 16 to 128, as said below
- tile_flow: int32 [8, 2048], P('flow', 'link'), may hold values from 0 to 1023
- tile_link: int32 [8, 2048], P('flow', 'link'), may hold values from 0 to 511, as said below
- flow_class: int32 [1048576], P('flow'), may hold values from 0 to 255
- class_weight: float32 [256], replicated, may hold values from 0.25 to 4
- access_price: float32 [1048576], P('flow'), may hold values from 0.5 to 4
- capacity: float32 [1048576], P('link'), may hold values from 1 to 8
- init_price: float32 [1048576], P('link'), may hold values from 0.5 to 2
Outputs:
- flow_rate: float32 [1048576], P('flow')
- link_price: float32 [1048576], P('link')
Inputs may be any that keep to these rules, and one draw needn't show every extreme that they name: `route_tiles`: entries are 0 or 1. `tile_count`: counts follow 128 divided by 1, 2, 4 or 8; some device uses all 128 slots in every draw. `tile_link`: within one device's slots no link block repeats.
All inputs are finite; a program needn't handle non-finite values.
Results may differ from a plain program's by a relative error of at most 0.0014.
Values may be sent and summed in bfloat16 or wider, within the bound.
No kernel may reach another device: no remote copies, remote signals or barrier semaphores. Data moves between devices by JAX's collectives and lax.ppermute only.
A program may use at most 64 MiB of HBM per device.

v0:
```python
import jax
import jax.numpy as jnp
from jax import lax
from jax.sharding import PartitionSpec as P

ITERS = 2
step_size = 0.5


def on_device(
    route_tiles,
    tile_count,
    tile_flow,
    tile_link,
    flow_class,
    class_weight,
    access_price,
    capacity,
    init_price,
):
    slots = route_tiles.shape[0]
    tile = route_tiles.shape[2]
    valid = (jnp.arange(slots, dtype=jnp.int32) < tile_count[0, 0]).astype(jnp.float32)
    flow_idx = tile_flow[0]
    link_idx = tile_link[0]
    flow_blocks = access_price.shape[0] // tile
    link_blocks = capacity.shape[0] // tile
    link_cap = capacity.reshape(link_blocks, tile)
    price = init_price.reshape(link_blocks, tile)
    weight = jnp.take(class_weight, flow_class).reshape(flow_blocks, tile)
    access = access_price.reshape(flow_blocks, tile)
    rate = jnp.zeros((flow_blocks, tile), jnp.float32)
    for step in range(ITERS):
        price_b = price.astype(jnp.bfloat16)
        picked = jnp.take(price_b, link_idx, axis=0)
        term = (
            jnp.einsum("sab,sa->sb", route_tiles, picked, preferred_element_type=jnp.float32)
            * valid[:, None]
        )
        route_part = jax.ops.segment_sum(term, flow_idx, num_segments=flow_blocks)
        route_sum = lax.psum(route_part, "link")
        rate = weight / (access + route_sum)
        rate_b = rate.astype(jnp.bfloat16)
        sent = jnp.take(rate_b, flow_idx, axis=0)
        term = (
            jnp.einsum("sab,sb->sa", route_tiles, sent, preferred_element_type=jnp.float32)
            * valid[:, None]
        )
        load_part = jax.ops.segment_sum(term, link_idx, num_segments=link_blocks)
        load = lax.psum(load_part, "flow")
        price = price * jnp.exp(step_size * (load / link_cap - 1.0))
    return (rate.reshape(-1), price.reshape(-1))


def solution(mesh):
    return jax.shard_map(
        on_device,
        mesh=mesh,
        in_specs=(
            P("flow", "link", None),
            P("flow", "link"),
            P("flow", "link"),
            P("flow", "link"),
            P("flow"),
            P(),
            P("flow"),
            P("link"),
            P("link"),
        ),
        out_specs=(P("flow"), P("link")),
        check_vma=False,
    )
```

profile of v0, /device:TPU:0, one launch (start us, length us, event | category | flops | bytes accessed | tf_op | source)
XLA Modules:
  0.0 1073.4 jit_solution(16845775853648401084)
XLA Ops:
  7.2 0.0 copy-start
  7.2 0.0 copy-start.1
  7.2 0.0 all-reduce.5.cloned.1.call-start
  7.2 0.7 compare_and_fusion
  8.0 0.0 copy-start.10
  8.0 0.7 compare_select_fusion.1
  9.3 0.0 copy-start.7
  9.3 0.0 copy-start.9
  9.3 1.0 bitcast_convert_fusion
  10.3 0.7 gather_fusion.1
  11.0 0.1 select_bitcast_fusion.3
  11.1 3.4 fusion.27
  14.5 2.0 scatter_custom_fusion
  16.5 0.0 all-reduce.5.cloned.1.call-update
  16.5 0.0 all-reduce.7.cloned.1.call-start
  16.5 0.0 copy-done.10
  16.5 0.0 copy-done.7
  16.6 0.0 copy-done.9
  16.6 0.0 copy-done.1
  16.6 0.1 fusion.3
  16.7 0.0 copy-done
  16.7 0.0 copy-start.12
  16.7 0.0 copy-start.2
  16.7 0.0 copy-start.4
  16.7 815.4 %gather_fusion = f32[131072]{0:T(1024)S(1)} fusion(f32[256]{0:T(256)S(1)} %copy-done, s32[131072]{0:T(1024)S(1)} %fusion.3), kind=kCustom, calls=%fused_computation.4 | custom fusion | bytes 1572864 | tf_op jit(solution)/shard_map/jit(_take)/gather | solution.py:30
  832.2 0.0 copy-done.12
  832.2 0.0 copy-start.8
  832.2 0.0 copy-start.3
  832.2 0.0 copy-start.5
  832.3 0.0 copy-start.11
  832.3 0.0 all-reduce.5.cloned.1.call-done
  832.3 0.0 copy-done.2
  832.3 0.0 copy-done.4
  832.3 1.3 fusion.1
  833.6 0.7 gather_fusion.2
  834.3 0.1 select_bitcast_fusion.2
  834.4 4.4 fusion.25
  838.9 0.0 copy-done.8
  838.9 1.9 scatter_custom_fusion.1
  840.8 0.0 all-reduce.7.cloned.1.call-update
  840.8 0.0 all-reduce.9.cloned.1.call-start
  840.9 63.0 %all-reduce.7.cloned.1.call-done = f32[512,128]{1,0:T(8,128)} async-done(((f32[512,128]{1,0:T(8,128)}), f32[512,128]{1,0:T(8,128)}) %all-reduce.7.cloned.1.call-update) | async-done | bytes 262160 | tf_op jit(solution)/shard_map/psum | solution.py:50
  903.8 0.0 copy-done.3
  903.8 0.0 copy-done.5
  903.8 1.0 fusion.37
  904.9 0.8 gather_fusion.3
  905.7 0.0 copy-done.11
  905.7 0.1 select_bitcast_fusion.1
  905.8 3.4 fusion.23
  909.2 1.9 scatter_custom_fusion.2
  911.0 0.0 all-reduce.9.cloned.1.call-update
  911.1 0.0 copy-start.6
  911.1 0.0 all-reduce.11.cloned.1.call-start
  911.1 84.9 %all-reduce.9.cloned.1.call-done = f32[1024,128]{1,0:T(8,128)} async-done(((f32[1024,128]{1,0:T(8,128)}), f32[1024,128]{1,0:T(8,128)}) %all-reduce.9.cloned.1.call-update) | async-done | bytes 524304 | tf_op jit(solution)/shard_map/psum | solution.py:41
  996.1 2.1 fusion.38
  998.1 0.7 gather_fusion.4
  998.8 0.1 select_bitcast_fusion
  998.9 4.4 fusion.21
  1003.4 1.9 scatter_custom_fusion.3
  1005.3 0.0 all-reduce.11.cloned.1.call-update
  1005.3 59.8 %all-reduce.11.cloned.1.call-done = f32[512,128]{1,0:T(8,128)} async-done(((f32[512,128]{1,0:T(8,128)}), f32[512,128]{1,0:T(8,128)}) %all-reduce.11.cloned.1.call-update) | async-done | bytes 262160 | tf_op jit(solution)/shard_map/psum | solution.py:50
  1065.1 0.0 copy-done.6
  1065.1 1.8 fusion.12
  (5 shorter events, 0.0 us)
Async XLA Ops:
  7.2 9.5 copy-start
  7.2 9.4 copy-start.1
  7.2 825.1 %all-reduce.5.cloned.1.call-start = ((), (), s32[]{:S(2)}) async-start(), calls=%async_computation | async-start | bytes 1048576 | tf_op jit(solution)/shard_map/psum | solution.py:41
  8.0 8.6 copy-start.10
  9.3 7.3 copy-start.7
  9.3 7.3 copy-start.9
  16.5 887.3 %all-reduce.7.cloned.1.call-start = ((), (), s32[]{:S(2)}) async-start(), calls=%async_computation.1 | async-start | bytes 524288 | tf_op jit(solution)/shard_map/psum | solution.py:50
  16.7 815.5 %copy-start.12 = (s32[1,128]{1,0:T(1,128)S(1)}, s32[1,128]{1,0:T(1,128)}, u32[]{:S(2)}) copy-start(s32[1,128]{1,0:T(1,128)} %param.15) | copy-start | bytes 1540
  16.7 815.6 %copy-start.2 = (s32[131072]{0:T(1024)S(1)}, s32[131072]{0:T(1024)}, u32[]{:S(2)}) copy-start(s32[131072]{0:T(1024)} %param.17) | copy-start | bytes 1572868
  16.7 815.6 %copy-start.4 = (f32[131072]{0:T(1024)S(1)}, f32[131072]{0:T(1024)}, u32[]{:S(2)}) copy-start(f32[131072]{0:T(1024)} %param.19) | copy-start | bytes 1572868
  832.2 6.7 copy-start.8
  832.2 71.6 %copy-start.3 = (f32[65536]{0:T(1024)S(1)}, f32[65536]{0:T(1024)}, u32[]{:S(2)}) copy-start(f32[65536]{0:T(1024)} %param.21) | copy-start | bytes 786436
  832.2 71.6 %copy-start.5 = (f32[65536]{0:T(1024)S(1)}, f32[65536]{0:T(1024)}, u32[]{:S(2)}) copy-start(f32[65536]{0:T(1024)} %param.20) | copy-start | bytes 786436
  832.3 73.4 %copy-start.11 = (pred[128]{0:T(512)(128)(4,1)S(1)}, pred[128]{0:T(512)(128)(4,1)}, u32[]{:S(2)}) copy-start(pred[128]{0:T(512)(128)(4,1)} %copy-done.10) | copy-start | bytes 388
  840.8 155.3 %all-reduce.9.cloned.1.call-start = ((), (), s32[]{:S(2)}) async-start(), calls=%async_computation.2 | async-start | bytes 1048576 | tf_op jit(solution)/shard_map/psum | solution.py:41
  911.1 154.0 %copy-start.6 = (f32[512,128]{1,0:T(8,128)S(1)}, f32[512,128]{1,0:T(8,128)}, u32[]{:S(2)}) copy-start(f32[512,128]{1,0:T(8,128)} %all-reduce.7.cloned.1.call-done) | copy-start | bytes 786436
  911.1 154.0 %all-reduce.11.cloned.1.call-start = ((), (), s32[]{:S(2)}) async-start(), calls=%async_computation.3 | async-start | bytes 524288 | tf_op jit(solution)/shard_map/psum | solution.py:50
Sparse Core Ops, SparseCore 0:
  16.6 88.2 all-reduce.4
  840.9 62.8 all-reduce.6
  911.2 84.8 all-reduce.8
  1005.4 59.6 all-reduce.10
where the time goes:
time: 1070 us
  local copies, waits for them, and re-layouts  818 us (76%)
  waiting for transfers between devices  208 us (19%)
  other arithmetic  16.7 us (2%)
  matrix products  15.6 us (1%)
  between operations  14.7 us (1%)
    gather x1, local copies, waits for them, and re-layouts, on_device(): weight = jnp.take(class_weight, flow_class).reshape(flow_blocks, tile)  815 us
    psum x2, waiting for transfers between devices, on_device(): load = lax.psum(load_part, 'flow')  123 us
    psum x2, waiting for transfers between devices, on_device(): route_sum = lax.psum(route_part, 'link')  85 us
  transfers between devices with their start and end apart: 4, of which 3 were waited for; matrix products, arithmetic and copies ran while one was open for 76% of the time, Pallas kernels for 0%

commit v1 on v0

--- a/solution.py
+++ b/solution.py
@@ -47,7 +47,7 @@
             * valid[:, None]
         )
         load_part = jax.ops.segment_sum(term, link_idx, num_segments=link_blocks)
-        load = lax.psum(load_part, "flow")
+        load = jnp.sum(lax.all_gather(load_part, "flow"), axis=0)
         price = price * jnp.exp(step_size * (load / link_cap - 1.0))
     return (rate.reshape(-1), price.reshape(-1))
 

time: 1070 us -> 1010 us (0.944)
  waiting for transfers between devices: 208 us -> 139 us
    psum x2 -> x0, waiting for transfers between devices: 123 us -> none  [on_device(): load = lax.psum(load_part, 'flow')]
    all_gather x0 -> x2, waiting for transfers between devices: none -> 52.7 us  [on_device(): load = jnp.sum(lax.all_gather(load_part, 'flow'), axis=0)]
  transfers between devices with their start and end apart: 4 -> 4, of which waited for: 3 -> 3; matrix products, arithmetic and copies ran while one was open for 76% -> 81% of each run, Pallas kernels for 0% -> 0%
where the time goes in v1:
time: 1010 us
  local copies, waits for them, and re-layouts  818 us (81%)
  waiting for transfers between devices  139 us (14%)
  other arithmetic  18.2 us (2%)
  matrix products  15.6 us (2%)
  between operations  14.7 us (1%)
    gather x1, local copies, waits for them, and re-layouts, on_device(): weight = jnp.take(class_weight, flow_class).reshape(flow_blocks, tile)  815 us
    psum x2, waiting for transfers between devices, on_device(): route_sum = lax.psum(route_part, 'link')  86.3 us
    all_gather x2, waiting for transfers between devices, on_device(): load = jnp.sum(lax.all_gather(load_part, 'flow'), axis=0)  52.7 us
  transfers between devices with their start and end apart: 4, of which 3 were waited for; matrix products, arithmetic and copies ran while one was open for 81% of the time, Pallas kernels for 0%

profile of v1, /device:TPU:0, one launch (start us, length us, event | category | flops | bytes accessed | tf_op | source)
XLA Modules:
  0.0 1006.2 jit_solution(5227960569146404172)
XLA Ops:
  7.2 0.0 copy-start
  7.2 0.0 copy-start.1
  7.2 0.0 all-reduce.3.cloned.1.call-start
  7.2 0.7 compare_and_fusion
  8.0 0.0 copy-start.9
  8.0 0.7 compare_select_fusion.1
  9.3 0.0 copy-start.6
  9.3 0.0 copy-start.8
  9.3 1.0 bitcast_convert_fusion
  10.3 0.7 gather_fusion.1
  11.0 0.1 select_bitcast_fusion.3
  11.1 3.4 fusion.31
  14.5 2.0 scatter_custom_fusion
  16.5 0.0 all-reduce.3.cloned.1.call-update
  16.5 0.0 all-gather.5.cloned.1.call-start
  16.5 0.0 copy-done.9
  16.5 0.0 copy-done.6
  16.6 0.0 copy-done.8
  16.6 0.0 copy-done.1
  16.6 0.1 fusion.3
  16.7 0.0 copy-done
  16.7 0.0 copy-start.11
  16.7 0.0 copy-start.2
  16.7 0.0 copy-start.4
  16.7 815.4 %gather_fusion = f32[131072]{0:T(1024)S(1)} fusion(f32[256]{0:T(256)S(1)} %copy-done, s32[131072]{0:T(1024)S(1)} %fusion.3), kind=kCustom, calls=%fused_computation.4 | custom fusion | bytes 1572864 | tf_op jit(solution)/shard_map/jit(_take)/gather | solution.py:30
  832.2 0.0 copy-done.11
  832.2 0.0 copy-start.7
  832.2 0.0 all-reduce.3.cloned.1.call-done
  832.3 0.0 copy-done.2
  832.3 0.0 copy-done.4
  832.3 1.3 fusion.1
  833.6 0.0 copy-start.3
  833.6 0.0 copy-start.5
  833.6 0.7 gather_fusion.2
  834.3 0.1 select_bitcast_fusion.2
  834.4 0.0 copy-start.10
  834.4 4.4 fusion.29
  838.8 0.0 copy-done.7
  838.8 1.9 scatter_custom_fusion.1
  840.7 0.0 all-gather.5.cloned.1.call-update
  840.8 0.0 all-reduce.5.cloned.1.call-start
  840.8 27.9 %all-gather.5.cloned.1.call-done = f32[4096,128]{1,0:T(8,128)} async-done(((f32[512,128]{1,0:T(8,128)}), f32[4096,128]{1,0:T(8,128)}) %all-gather.5.cloned.1.call-update) | async-done | bytes 2097168 | tf_op jit(solution)/shard_map/all_gather | solution.py:50
  868.7 1.7 reduce_sum.22
  870.4 0.0 copy-done.3
  870.5 0.0 copy-done.5
  870.5 0.1 fusion.20
  870.6 0.8 gather_fusion.3
  871.4 0.0 copy-done.10
  871.4 0.1 select_bitcast_fusion.1
  871.5 3.4 fusion.27
  874.9 1.9 scatter_custom_fusion.2
  876.7 0.0 all-reduce.5.cloned.1.call-update
  876.8 0.0 all-gather.7.cloned.1.call-start
  876.8 86.3 %all-reduce.5.cloned.1.call-done = f32[1024,128]{1,0:T(8,128)} async-done(((f32[1024,128]{1,0:T(8,128)}), f32[1024,128]{1,0:T(8,128)}) %all-reduce.5.cloned.1.call-update) | async-done | bytes 524304 | tf_op jit(solution)/shard_map/psum | solution.py:41
  963.1 2.1 fusion.41
  965.1 0.7 gather_fusion.4
  965.8 0.1 select_bitcast_fusion
  965.9 4.4 fusion.25
  970.4 1.9 scatter_custom_fusion.3
  972.3 0.0 all-gather.7.cloned.1.call-update
  972.3 24.8 %all-gather.7.cloned.1.call-done = f32[4096,128]{1,0:T(8,128)} async-done(((f32[512,128]{1,0:T(8,128)}), f32[4096,128]{1,0:T(8,128)}) %all-gather.7.cloned.1.call-update) | async-done | bytes 2097168 | tf_op jit(solution)/shard_map/all_gather | solution.py:50
  997.1 1.7 reduce_sum.24
  998.8 0.8 fusion.7
  (5 shorter events, 0.0 us)
Async XLA Ops:
  7.2 9.5 copy-start
  7.2 9.4 copy-start.1
  7.2 825.1 %all-reduce.3.cloned.1.call-start = ((), (), s32[]{:S(2)}) async-start(), calls=%async_computation | async-start | bytes 1048576 | tf_op jit(solution)/shard_map/psum | solution.py:41
  8.0 8.6 copy-start.9
  9.3 7.3 copy-start.6
  9.3 7.3 copy-start.8
  16.5 852.2 %all-gather.5.cloned.1.call-start = ((), (), s32[]{:S(2)}) async-start(), calls=%async_computation.2 | async-start | bytes 2359296 | tf_op jit(solution)/shard_map/all_gather | solution.py:50
  16.7 815.5 %copy-start.11 = (s32[1,128]{1,0:T(1,128)S(1)}, s32[1,128]{1,0:T(1,128)}, u32[]{:S(2)}) copy-start(s32[1,128]{1,0:T(1,128)} %param.15) | copy-start | bytes 1540
  16.7 815.5 %copy-start.2 = (s32[131072]{0:T(1024)S(1)}, s32[131072]{0:T(1024)}, u32[]{:S(2)}) copy-start(s32[131072]{0:T(1024)} %param.17) | copy-start | bytes 1572868
  16.7 815.5 %copy-start.4 = (f32[131072]{0:T(1024)S(1)}, f32[131072]{0:T(1024)}, u32[]{:S(2)}) copy-start(f32[131072]{0:T(1024)} %param.19) | copy-start | bytes 1572868
  832.2 6.6 copy-start.7
  833.6 36.9 %copy-start.3 = (f32[65536]{0:T(1024)S(1)}, f32[65536]{0:T(1024)}, u32[]{:S(2)}) copy-start(f32[65536]{0:T(1024)} %param.21) | copy-start | bytes 786436
  833.6 36.9 %copy-start.5 = (f32[65536]{0:T(1024)S(1)}, f32[65536]{0:T(1024)}, u32[]{:S(2)}) copy-start(f32[65536]{0:T(1024)} %param.20) | copy-start | bytes 786436
  834.4 37.0 %copy-start.10 = (pred[128]{0:T(512)(128)(4,1)S(1)}, pred[128]{0:T(512)(128)(4,1)}, u32[]{:S(2)}) copy-start(pred[128]{0:T(512)(128)(4,1)} %copy-done.9) | copy-start | bytes 388
  840.8 122.3 %all-reduce.5.cloned.1.call-start = ((), (), s32[]{:S(2)}) async-start(), calls=%async_computation.1 | async-start | bytes 1048576 | tf_op jit(solution)/shard_map/psum | solution.py:41
  876.8 120.4 %all-gather.7.cloned.1.call-start = ((), (), s32[]{:S(2)}) async-start(), calls=%async_computation.3 | async-start | bytes 2359296 | tf_op jit(solution)/shard_map/all_gather | solution.py:50
Sparse Core Ops, SparseCore 0:
  16.6 88.2 all-reduce.2
  840.9 27.7 all-gather.4
  876.9 86.1 all-reduce.4
  972.4 24.6 all-gather.6
